TPU v7x, 512 devices: a whole 4x4x16 slice. The times are simulated.
512 devices in a mesh: row: 16 (over x_lo, y, core), col: 32 (over x_hi, z).
Axes of the slice: x: 4 (x_hi: 2, x_lo: 2; x = x_hi * 2 + x_lo), y: 4, z: 16, core: 2. Of those that a mesh axis runs over, the one named last changes fastest.
Arguments:
- inverse_slab: bfloat16 [65536, 8192], P('row', 'col'), may hold values from -0.0234375 to 0.0234375
- cot_solved: bfloat16 [64, 65536], P(None, ('row', 'col')), may hold values from -6 to 6
- cot_direct: bfloat16 [64, 8192], P(None, 'col'), may hold values from -6 to 6
- solved_panel: bfloat16 [64, 65536], P(None, 'col'), may hold values from -1.078125 to 1.078125
Outputs:
- grad_factor: float32 [64, 8192], P(None, 'col')
- grad_operator: bfloat16 [8192, 65536], P('row', 'col')
All inputs are finite; a program needn't handle non-finite values.
Results may differ from a plain program's by a relative error of at most 0.0049.
Values may be sent and summed in bfloat16 or wider, within the bound.
No kernel may reach another device: no remote copies, remote signals or barrier semaphores. Data moves between devices by JAX's collectives and lax.ppermute only.
A program may use at most 64 MiB of HBM per device.

v0:
```python
import jax
import jax.numpy as jnp
from jax import lax
from jax.sharding import PartitionSpec as P


def body(inverse_slab, cot_solved, cot_direct, solved_panel):
    scale = 1.0 / jnp.sqrt(jnp.float32(2.0))
    block_rows = lax.all_gather(cot_solved, "col", axis=1, tiled=True)
    partial_sum = jnp.dot(block_rows, inverse_slab, preferred_element_type=jnp.float32)
    pulled = lax.psum(partial_sum, "row")
    grad_factor = (cot_direct.astype(jnp.float32) + pulled) * scale
    pulled_low = pulled.astype(jnp.bfloat16)
    width = pulled_low.shape[1]
    factor = lax.axis_size("col") // lax.axis_size("row")
    gathered = lax.all_gather(pulled_low, "col", axis=1, tiled=True)
    offset = lax.axis_index("row") * (factor * width)
    needed = lax.dynamic_slice_in_dim(gathered, offset, factor * width, 1)
    product = lax.dot_general(
        needed, solved_panel, (((0,), (0,)), ((), ())), preferred_element_type=jnp.float32
    )
    grad_operator = (product * -scale).astype(jnp.bfloat16)
    return (grad_factor, grad_operator)


def solution(mesh):
    in_specs = (P("row", "col"), P(None, ("row", "col")), P(None, "col"), P(None, "col"))
    out_specs = (P(None, "col"), P("row", "col"))
    return jax.shard_map(body, mesh=mesh, in_specs=in_specs, out_specs=out_specs, check_vma=False)
```

profile of v0, /device:TPU:8, one launch (start us, length us, event | category | flops | bytes accessed | tf_op | source)
XLA Modules:
  0.0 356.7 jit_solution(521984565598067549)
XLA Ops:
  7.2 0.0 copy-start
  7.2 0.0 copy-start.2
  7.2 0.0 copy-start.1
  7.2 0.0 all-reduce.2.cloned.1.call-start
  7.2 85.5 %all_gather.6 = bf16[64,4096]{1,0:T(8,128)(2,1)S(1)} all-gather(bf16[64,128]{1,0:T(8,128)(2,1)} %param.5), channel_id=1, replica_groups=mesh['row'=16,'col'=32] {'col'}, dimensions={1}, use_global_device_ids=true | all-gather | bytes 540672 | tf_op jit(solution)/shard_map/all_gather | solution.py:9
  92.8 0.0 copy-done
  92.8 1.1 fusion.3
  93.8 0.0 all-reduce.2.cloned.1.call-update
  93.9 0.0 all-gather.2.cloned.1.call-start
  93.9 111.6 %all-reduce.2.cloned.1.call-done = f32[64,256]{1,0:T(8,128)} async-done(((f32[64,256]{1,0:T(8,128)}), f32[64,256]{1,0:T(8,128)}) %all-reduce.2.cloned.1.call-update) | async-done | bytes 65552 | tf_op jit(solution)/shard_map/psum | solution.py:11
  205.6 0.0 copy-done.2
  205.6 1.6 fusion.2
  207.1 0.0 all-gather.2.cloned.1.call-update
  207.1 139.8 %all-gather.2.cloned.1.call-done = bf16[64,8192]{1,0:T(8,128)(2,1)} async-done(((bf16[64,256]{1,0:T(8,128)(2,1)}), bf16[64,8192]{1,0:T(8,128)(2,1)}) %all-gather.2.cloned.1.call-update) | async-done | bytes 1048592 | tf_op jit(solution)/shard_map/all_gather | solution.py:16
  347.0 0.0 copy-done.1
  347.0 2.9 multiply_convert_fusion
Async XLA Ops:
  7.2 85.6 %copy-start = (bf16[4096,256]{1,0:T(8,128)(2,1)S(1)}, bf16[4096,256]{1,0:T(8,128)(2,1)}, u32[]{:S(2)}) copy-start(bf16[4096,256]{1,0:T(8,128)(2,1)} %param.4) | copy-start | bytes 6291460
  7.2 198.4 %copy-start.2 = (bf16[64,256]{1,0:T(8,128)(2,1)S(1)}, bf16[64,256]{1,0:T(8,128)(2,1)}, u32[]{:S(2)}) copy-start(bf16[64,256]{1,0:T(8,128)(2,1)} %param.6) | copy-start | bytes 98308
  7.2 339.8 %copy-start.1 = (bf16[64,2048]{1,0:T(8,128)(2,1)S(1)}, bf16[64,2048]{1,0:T(8,128)(2,1)}, u32[]{:S(2)}) copy-start(bf16[64,2048]{1,0:T(8,128)(2,1)} %param.7) | copy-start | bytes 786436
  7.2 198.4 %all-reduce.2.cloned.1.call-start = ((), (), s32[]{:S(2)}) async-start(), calls=%async_computation | async-start | bytes 131072 | tf_op jit(solution)/shard_map/psum | solution.py:11
  93.9 253.1 %all-gather.2.cloned.1.call-start = ((), (), s32[]{:S(2)}) async-start(), calls=%async_computation.1 | async-start | bytes 1081344 | tf_op jit(solution)/shard_map/all_gather | solution.py:16
Sparse Core Ops, SparseCore 0:
  94.0 111.5 all-reduce.1
  209.0 137.8 all-gather.1
where the time goes:
time: 357 us
  waiting for transfers between devices  251 us (70%)
  blocking collectives  85.5 us (24%)
  between operations  14.1 us (4%)
  matrix products  3.98 us (1%)
    all_gather x1, waiting for transfers between devices, body(): gathered = lax.all_gather(pulled_low, 'col', axis=1, tiled=True)  140 us
    psum x1, waiting for transfers between devices, body(): pulled = lax.psum(partial_sum, 'row')  112 us
    all_gather x1, blocking collectives, body(): block_rows = lax.all_gather(cot_solved, 'col', axis=1, tiled=True)  85.5 us
  transfers between devices with their start and end apart: 2, of which 2 were waited for; matrix products, arithmetic and copies ran while one was open for 0% of the time, Pallas kernels for 0%

commit v1 on v0

--- a/solution.py
+++ b/solution.py
@@ -8,7 +8,8 @@
     scale = 1.0 / jnp.sqrt(jnp.float32(2.0))
     block_rows = lax.all_gather(cot_solved, "col", axis=1, tiled=True)
     partial_sum = jnp.dot(block_rows, inverse_slab, preferred_element_type=jnp.float32)
-    pulled = lax.psum(partial_sum, "row")
+    shards = lax.all_gather(partial_sum, "row")
+    pulled = jnp.sum(shards, axis=0)
     grad_factor = (cot_direct.astype(jnp.float32) + pulled) * scale
     pulled_low = pulled.astype(jnp.bfloat16)
     width = pulled_low.shape[1]

time: 357 us -> 272 us (0.76)
  waiting for transfers between devices: 251 us -> 167 us
    psum x1 -> x0, waiting for transfers between devices: 112 us -> none  [body(): pulled = lax.psum(partial_sum, 'row')]
    all_gather x0 -> x1, waiting for transfers between devices: none -> 28.8 us  [body(): shards = lax.all_gather(partial_sum, 'row')]
where the time goes in v1:
time: 272 us
  waiting for transfers between devices  167 us (61%)
  blocking collectives  85.5 us (31%)
  between operations  14.1 us (5%)
  matrix products  3.97 us (1%)
    all_gather x1, waiting for transfers between devices, body(): gathered = lax.all_gather(pulled_low, 'col', axis=1, tiled=True)  138 us
    all_gather x1, blocking collectives, body(): block_rows = lax.all_gather(cot_solved, 'col', axis=1, tiled=True)  85.5 us
    all_gather x1, waiting for transfers between devices, body(): shards = lax.all_gather(partial_sum, 'row')  28.8 us
  transfers between devices with their start and end apart: 2, of which 2 were waited for; matrix products, arithmetic and copies ran while one was open for 0% of the time, Pallas kernels for 0%

profile of v1, /device:TPU:8, one launch (start us, length us, event | category | flops | bytes accessed | tf_op | source)
XLA Modules:
  0.0 272.2 jit_solution(1675115861001552905)
XLA Ops:
  7.2 0.0 copy-start
  7.2 0.0 copy-start.2
  7.2 0.0 all-gather.6.cloned.1.call-start
  7.2 85.5 %all_gather.12 = bf16[64,4096]{1,0:T(8,128)(2,1)S(1)} all-gather(bf16[64,128]{1,0:T(8,128)(2,1)} %param.5), channel_id=1, replica_groups=mesh['row'=16,'col'=32] {'col'}, dimensions={1}, use_global_device_ids=true | all-gather | bytes 540672 | tf_op jit(solution)/shard_map/all_gather | solution.py:9
  92.7 0.0 copy-done
  92.7 0.0 copy-start.1
  92.7 1.1 fusion.3
  93.8 0.0 all-gather.6.cloned.1.call-update
  93.9 0.0 all-gather.4.cloned.1.call-start
  93.9 28.8 %all-gather.6.cloned.1.call-done = f32[1024,256]{1,0:T(8,128)} async-done(((f32[64,256]{1,0:T(8,128)}), f32[1024,256]{1,0:T(8,128)}) %all-gather.6.cloned.1.call-update) | async-done | bytes 1048592 | tf_op jit(solution)/shard_map/all_gather | solution.py:11
  122.8 1.3 reduce_sum.9
  124.0 0.0 copy-done.2
  124.1 0.7 fusion.2
  124.7 0.0 all-gather.4.cloned.1.call-update
  124.7 137.7 %all-gather.4.cloned.1.call-done = bf16[64,8192]{1,0:T(8,128)(2,1)} async-done(((bf16[64,256]{1,0:T(8,128)(2,1)}), bf16[64,8192]{1,0:T(8,128)(2,1)}) %all-gather.4.cloned.1.call-update) | async-done | bytes 1048592 | tf_op jit(solution)/shard_map/all_gather | solution.py:17
  262.5 0.0 copy-done.1
  262.5 2.9 %multiply_convert_fusion = bf16[512,2048]{1,0:T(8,128)(2,1)} fusion(bf16[64,2048]{1,0:T(8,128)(2,1)S(1)} %copy-done.1, bf16[64,8192]{1,0:T(8,128)(2,1)} %all-gather.4.cloned.1.call-done, s32[]{:T(128)S(6)} %select_n.3), kind=kOutput, calls=%fused_computation | convolution fusion | flops 136314880 | bytes 2424836 | tf_op jit(solution)/shard_map/dot_general | solution.py:20
Async XLA Ops:
  7.2 85.6 %copy-start = (bf16[4096,256]{1,0:T(8,128)(2,1)S(1)}, bf16[4096,256]{1,0:T(8,128)(2,1)}, u32[]{:S(2)}) copy-start(bf16[4096,256]{1,0:T(8,128)(2,1)} %param.4) | copy-start | bytes 6291460
  7.2 116.9 %copy-start.2 = (bf16[64,256]{1,0:T(8,128)(2,1)S(1)}, bf16[64,256]{1,0:T(8,128)(2,1)}, u32[]{:S(2)}) copy-start(bf16[64,256]{1,0:T(8,128)(2,1)} %param.6) | copy-start | bytes 98308
  7.2 115.6 %all-gather.6.cloned.1.call-start = ((), (), s32[]{:S(2)}) async-start(), calls=%async_computation.1 | async-start | bytes 1114112 | tf_op jit(solution)/shard_map/all_gather | solution.py:11
  92.7 169.7 %copy-start.1 = (bf16[64,2048]{1,0:T(8,128)(2,1)S(1)}, bf16[64,2048]{1,0:T(8,128)(2,1)}, u32[]{:S(2)}) copy-start(bf16[64,2048]{1,0:T(8,128)(2,1)} %param.7) | copy-start | bytes 786436
  93.9 168.6 %all-gather.4.cloned.1.call-start = ((), (), s32[]{:S(2)}) async-start(), calls=%async_computation | async-start | bytes 1081344 | tf_op jit(solution)/shard_map/all_gather | solution.py:17
Sparse Core Ops, SparseCore 0:
  94.0 28.7 all-gather.5
  126.2 136.1 all-gather.3

commit v2 on v0

--- a/solution.py
+++ b/solution.py
@@ -6,7 +6,8 @@
 
 def body(inverse_slab, cot_solved, cot_direct, solved_panel):
     scale = 1.0 / jnp.sqrt(jnp.float32(2.0))
-    block_rows = lax.all_gather(cot_solved, "col", axis=1, tiled=True)
+    sent = jnp.stack([cot_solved] * lax.axis_size("col"))
+    block_rows = jnp.concatenate(lax.all_to_all(sent, "col", 0, 0), axis=1)
     partial_sum = jnp.dot(block_rows, inverse_slab, preferred_element_type=jnp.float32)
     pulled = lax.psum(partial_sum, "row")
     grad_factor = (cot_direct.astype(jnp.float32) + pulled) * scale

time: 357 us -> 325 us (0.910)
  blocking collectives: 85.5 us -> 50.5 us
    all_gather x1 -> x0, blocking collectives: 85.5 us -> none  [body(): block_rows = lax.all_gather(cot_solved, 'col', axis=1, tiled=True)]
    all_to_all x0 -> x1, blocking collectives: none -> 50.5 us  [body(): block_rows = jnp.concatenate(lax.all_to_all(sent, 'col', 0, 0), axis=1)]
where the time goes in v2:
time: 325 us
  waiting for transfers between devices  254 us (78%)
  blocking collectives  50.5 us (16%)
  between operations  14.1 us (4%)
  matrix products  4 us (1%)
    all_gather x1, waiting for transfers between devices, body(): gathered = lax.all_gather(pulled_low, 'col', axis=1, tiled=True)  140 us
    psum x1, waiting for transfers between devices, body(): pulled = lax.psum(partial_sum, 'row')  114 us
    all_to_all x1, blocking collectives, body(): block_rows = jnp.concatenate(lax.all_to_all(sent, 'col', 0, 0), axis=1)  50.5 us
  transfers between devices with their start and end apart: 2, of which 2 were waited for; matrix products, arithmetic and copies ran while one was open for 0% of the time, Pallas kernels for 0%

profile of v2, /device:TPU:8, one launch (start us, length us, event | category | flops | bytes accessed | tf_op | source)
XLA Modules:
  0.0 325.2 jit_solution(10761793197826677998)
XLA Ops:
  7.2 0.0 copy-start
  7.2 0.0 copy-start.2
  7.2 0.0 all-reduce.2.cloned.1.call-start
  7.2 1.0 stack.2
  8.2 0.0 copy-start.1
  8.2 50.5 %all_to_all.5 = bf16[32,64,128]{2,1,0:T(8,128)(2,1)S(1)} all-to-all(bf16[32,64,128]{2,1,0:T(8,128)(2,1)S(1)} %stack.2), channel_id=1, replica_groups=mesh['row'=16,'col'=32] {'col'}, dimensions={0} | all-to-all | bytes 1048576 | tf_op jit(solution)/shard_map/all_to_all | solution.py:10
  58.8 0.0 copy-done
  58.8 1.1 fusion
  59.9 0.0 all-reduce.2.cloned.1.call-update
  59.9 0.0 all-gather.2.cloned.1.call-start
  59.9 114.2 %all-reduce.2.cloned.1.call-done = f32[64,256]{1,0:T(8,128)} async-done(((f32[64,256]{1,0:T(8,128)}), f32[64,256]{1,0:T(8,128)}) %all-reduce.2.cloned.1.call-update) | async-done | bytes 65552 | tf_op jit(solution)/shard_map/psum | solution.py:12
  174.1 0.0 copy-done.2
  174.1 1.6 fusion.5
  175.7 0.0 all-gather.2.cloned.1.call-update
  175.7 139.8 %all-gather.2.cloned.1.call-done = bf16[64,8192]{1,0:T(8,128)(2,1)} async-done(((bf16[64,256]{1,0:T(8,128)(2,1)}), bf16[64,8192]{1,0:T(8,128)(2,1)}) %all-gather.2.cloned.1.call-update) | async-done | bytes 1048592 | tf_op jit(solution)/shard_map/all_gather | solution.py:17
  315.5 0.0 copy-done.1
  315.5 2.9 multiply_convert_fusion
Async XLA Ops:
  7.2 51.6 %copy-start = (bf16[4096,256]{1,0:T(8,128)(2,1)S(1)}, bf16[4096,256]{1,0:T(8,128)(2,1)}, u32[]{:S(2)}) copy-start(bf16[4096,256]{1,0:T(8,128)(2,1)} %param.4) | copy-start | bytes 6291460
  7.2 166.9 %copy-start.2 = (bf16[64,256]{1,0:T(8,128)(2,1)S(1)}, bf16[64,256]{1,0:T(8,128)(2,1)}, u32[]{:S(2)}) copy-start(bf16[64,256]{1,0:T(8,128)(2,1)} %param.6) | copy-start | bytes 98308
  7.2 166.9 %all-reduce.2.cloned.1.call-start = ((), (), s32[]{:S(2)}) async-start(), calls=%async_computation.1 | async-start | bytes 131072 | tf_op jit(solution)/shard_map/psum | solution.py:12
  8.2 307.3 %copy-start.1 = (bf16[64,2048]{1,0:T(8,128)(2,1)S(1)}, bf16[64,2048]{1,0:T(8,128)(2,1)}, u32[]{:S(2)}) copy-start(bf16[64,2048]{1,0:T(8,128)(2,1)} %param.7) | copy-start | bytes 786436
  59.9 255.6 %all-gather.2.cloned.1.call-start = ((), (), s32[]{:S(2)}) async-start(), calls=%async_computation.2 | async-start | bytes 1081344 | tf_op jit(solution)/shard_map/all_gather | solution.py:17
Sparse Core Ops, SparseCore 0:
  60.0 114.0 all-reduce.1
  177.6 137.8 all-gather.1
